TPU v7x, 256 devices: a whole 4x4x8 slice. The times are simulated.
256 devices in a mesh: sec: 32 (over z, y), blk: 8 (over x, core).
Axes of the slice: x: 4, y: 4, z: 8, core: 2. Of those that a mesh axis runs over, the one named last changes fastest.
Arguments:
- state_now: float32 [128, 65536], P(None, ('sec', 'blk')), may hold values from -5 to 5
- source: float32 [128, 65536], P(None, ('sec', 'blk')), may hold values from -6 to 6
- fan_gain: float32 [65536], P(('sec', 'blk')), may hold values from 0.5 to 12
- section_block: bfloat16 [65536, 2048], P(('sec', 'blk')), may hold values from -1 to 7
- block_inverse: bfloat16 [65536, 2048], P(('sec', 'blk')), may hold values from -1 to 1
- back_panel: bfloat16 [65536, 128], P(('sec', 'blk')), may hold values from -6 to 6
- ahead_panel: bfloat16 [65536, 128], P(('sec', 'blk')), may hold values from -0.0625 to 0.0625
- interface: int32 [32, 128], P('sec'), may hold values from 0 to 2047, as said below
Outputs:
- new_state: float32 [128, 65536], P(None, ('sec', 'blk'))
Inputs may be any that keep to these rules, and one draw needn't show every extreme that they name: `interface`: entries of one section are distinct; entry p lies in [p * 16, (p + 1) * 16).
All inputs are finite; a program needn't handle non-finite values.
Results may differ from a plain program's by a relative error of at most 0.0063.
Values may be sent and summed in bfloat16 or wider, within the bound.
A program may use at most 64 MiB of HBM per device.

v0:
```python
import jax
import jax.numpy as jnp
from jax import lax
from jax.sharding import PartitionSpec as P

KRYLOV = 3
epsilon = 1e-06


def extended(x, sides, width):
    for axis, dim in sides:
        size, length = (lax.axis_size(axis), x.shape[dim])
        up = [(i, (i + 1) % size) for i in range(size - 1)]
        down = [(j, i) for i, j in up]
        last = lax.slice_in_dim(x, length - width, length, axis=dim)
        first = lax.slice_in_dim(x, 0, width, axis=dim)
        before = lax.ppermute(last, axis, up)
        after = lax.ppermute(first, axis, down)
        x = jnp.concatenate([before, x, after], axis=dim)
    return x


def entering(value, axis, join, neutral):
    count, mine = (lax.axis_size(axis), lax.axis_index(axis))
    pieces = jax.tree.map(lambda part: lax.all_gather(part, axis), value)
    so_far = jax.tree.map(
        lambda part, zero: jnp.full_like(part, 0) + jnp.asarray(zero, part.dtype), value, neutral
    )

    def step(position, so_far):
        longer = join(so_far, jax.tree.map(lambda part: part[position], pieces))
        return jax.tree.map(lambda new, old: jnp.where(position < mine, new, old), longer, so_far)

    return lax.fori_loop(0, count - 1, step, so_far)


def least_squares(hessen, beta):
    cases = hessen.shape[0]
    depth = hessen.shape[2]
    rhs = jnp.zeros((cases, depth + 1), jnp.float32).at[:, 0].set(beta)
    upper = hessen
    for column in range(depth):
        upper_row = upper[:, column, :]
        lower_row = upper[:, column + 1, :]
        radius = jnp.sqrt(upper_row[:, column] ** 2 + lower_row[:, column] ** 2)
        cosine = upper_row[:, column] / radius
        sine_term = lower_row[:, column] / radius
        upper = upper.at[:, column, :].set(
            cosine[:, None] * upper_row + sine_term[:, None] * lower_row
        )
        upper = upper.at[:, column + 1, :].set(
            -sine_term[:, None] * upper_row + cosine[:, None] * lower_row
        )
        first_rhs = rhs[:, column]
        second_rhs = rhs[:, column + 1]
        rhs = rhs.at[:, column].set(cosine * first_rhs + sine_term * second_rhs)
        rhs = rhs.at[:, column + 1].set(-sine_term * first_rhs + cosine * second_rhs)
    weights = jnp.zeros((cases, depth), jnp.float32)
    for column in reversed(range(depth)):
        remain = rhs[:, column] - jnp.sum(
            upper[:, column, column + 1 :] * weights[:, column + 1 :], axis=1
        )
        weights = weights.at[:, column].set(remain / upper[:, column, column])
    return weights


def local(
    state_now, source, fan_gain, section_block, block_inverse, back_panel, ahead_panel, interface
):
    highest = lax.Precision.HIGHEST
    cases, node_rows = state_now.shape
    panel_width = back_panel.shape[1]
    indices = interface[0]
    first_row = lax.axis_index("blk") * node_rows
    selector = (indices[None, :] == first_row + jnp.arange(node_rows)[:, None]).astype(jnp.float32)
    contract = (((1,), (1,)), ((), ()))
    gain_panel = jnp.dot(
        block_inverse,
        lax.all_gather(back_panel, "blk", axis=0, tiled=True),
        preferred_element_type=jnp.float32,
    )
    panel_maps = -lax.psum(jnp.dot(selector.T, gain_panel, precision=highest), "blk")

    def section_terms(dense_part, behind_vals, piece):
        width = piece.shape[1]
        dense_part = lax.dot_general(
            piece, section_block, contract, preferred_element_type=jnp.float32
        )
        picker = (indices[None, :] == jnp.arange(width)[:, None]).astype(jnp.bfloat16)
        behind_vals = jnp.dot(piece, picker, preferred_element_type=jnp.float32)
        return (dense_part, behind_vals)

    def fold_section(carry, piece):
        return section_terms(carry[0], carry[1], piece)

    def operator(vector):
        rounded = vector.astype(jnp.bfloat16)
        empty_dense = jnp.zeros((cases, node_rows), jnp.float32)
        empty_panel = jnp.zeros((cases, panel_width), jnp.float32)
        start_carry = (empty_dense, empty_panel)
        folded = fold_section(start_carry, lax.all_gather(rounded, "blk", axis=1, tiled=True))
        dense_part, behind_vals = folded
        upward = lax.psum(jnp.dot(rounded, ahead_panel, preferred_element_type=jnp.float32), "blk")
        framed = extended(jnp.stack([behind_vals, upward])[None], (("sec", 0),), 1)
        behind = framed[0, 0].astype(jnp.bfloat16)
        ahead_term = framed[2, 1]
        lower_term = lax.dot_general(
            behind, back_panel, contract, preferred_element_type=jnp.float32
        )
        upper_term = jnp.dot(ahead_term, selector.T, precision=highest)
        return dense_part + lower_term + upper_term

    def compose(earlier, later):
        first_map, first_value = earlier
        second_map, second_value = later
        joined_map = jnp.dot(second_map, first_map, precision=highest)
        joined_value = jnp.dot(first_value, second_map.T, precision=highest) + second_value
        return (joined_map, joined_value)

    def lengths(vector):
        return jnp.sqrt(lax.psum(jnp.sum(vector * vector, axis=1), ("sec", "blk")) + epsilon)

    bent = jnp.tanh(state_now)
    residual = source - operator(state_now) - fan_gain[None, :] * bent
    jac_diag = fan_gain[None, :] * (1.0 - bent * bent)
    beta = lengths(residual)
    basis = [residual / beta[:, None]]
    directions = []
    hessen = jnp.zeros((cases, KRYLOV + 1, KRYLOV), jnp.float32)
    for column in range(KRYLOV):
        precondition_rounded = basis[column].astype(jnp.bfloat16)
        precondition_folded = lax.dot_general(
            lax.all_gather(precondition_rounded, "blk", axis=1, tiled=True),
            block_inverse,
            contract,
            preferred_element_type=jnp.float32,
        )
        values = lax.psum(jnp.dot(precondition_folded, selector, precision=highest), "blk")
        identity = (
            jnp.eye(panel_width, dtype=jnp.float32),
            jnp.zeros((cases, panel_width), jnp.float32),
        )
        _, before = entering((panel_maps, values), "sec", compose, identity)
        direction = precondition_folded - lax.dot_general(
            before, gain_panel, contract, precision=highest
        )
        product = operator(direction) + jac_diag * direction
        stacked = jnp.stack(basis)
        projections = lax.psum(jnp.sum(product[None] * stacked, axis=2), ("sec", "blk"))
        product = product - jnp.sum(projections[:, :, None] * stacked, axis=0)
        length = lengths(product)
        hessen = hessen.at[:, : column + 1, column].set(projections.T)
        hessen = hessen.at[:, column + 1, column].set(length)
        basis.append(product / length[:, None])
        directions.append(direction)
    weights = least_squares(hessen, beta)
    update = jnp.zeros_like(state_now)
    for column in range(KRYLOV):
        update = update + weights[:, column : column + 1] * directions[column]
    return state_now + update


def solution(mesh):
    in_specs = (
        P(None, ("sec", "blk")),
        P(None, ("sec", "blk")),
        P(("sec", "blk")),
        P(("sec", "blk"), None),
        P(("sec", "blk"), None),
        P(("sec", "blk"), None),
        P(("sec", "blk"), None),
        P("sec", None),
    )
    out_specs = P(None, ("sec", "blk"))
    return jax.shard_map(local, mesh=mesh, in_specs=in_specs, out_specs=out_specs, check_vma=False)
```

profile of v0, /device:TPU:1, one launch (start us, length us, event | category | flops | bytes accessed | tf_op | source)
XLA Modules:
  0.0 1640.1 jit_solution(12427240941463223437)
XLA Ops:
  6.5 1.1 convert_element_type.42
  7.6 1.7 convolution_bitcast_fusion.13
  9.4 16.2 all_gather.52
  27.1 13.1 all_gather.54
  40.7 34.6 %all-reduce.11.cloned.1.call-done = f32[1,128,128]{1,2,0:T(8,128)} async-done(((f32[1,128,128]{1,2,0:T(8,128)}), f32[1,128,128]{1,2,0:T(8,128)}) %all-reduce.11.cloned.1.call-update) | async-done | bytes 65552 | tf_op jit(solution)/shard_map/psum | solution.py:103
  76.1 3.1 collective-permute-start
  80.2 1.3 collective-permute-start.1
  81.7 4.2 collective-permute-done.1
  86.3 83.2 %psum.106 = f32[128]{0:T(128)S(1)} all-reduce(f32[128]{0:T(128)S(1)} %get-tuple-element.720), channel_id=1, replica_groups=mesh['sec'=32,'blk'=8] {'sec','blk'}, use_global_device_ids=true, to_apply=%region_4.0 | all-reduce | flops 128 | bytes 1024 | tf_op jit(solution)/shard_map/psum | solution.py:121
  169.7 13.9 all_gather.53
  185.0 57.8 %all-reduce.23.cloned.1.call-done = (f32[128,128]{1,0:T(8,128)}, f32[1,128,128]{2,1,0:T(8,128)}) async-done(((f32[128,128]{1,0:T(8,128)}, f32[1,128,128]{2,1,0:T(8,128)}), (f32[128,128]{1,0:T(8,128)}, f32[1,128,128]{2,1,0:T(8,128)})) %all-reduce.23.cloned.1.call-update) | async-done | bytes 131088 | tf_op jit(solution)/shard_map/psum | solution.py:82
  242.8 1.5 neg.24
  244.9 75.7 %all-gather.12.cloned.1.call-done = f32[4096,128]{1,0:T(8,128)} async-done(((f32[128,128]{1,0:T(8,128)}), f32[4096,128]{1,0:T(8,128)}) %all-gather.12.cloned.1.call-update) | async-done | bytes 2097168 | tf_op jit(solution)/shard_map/all_gather | solution.py:25
  320.6 77.6 %all-gather.6.cloned.1.call-done = f32[32,128,128]{2,1,0:T(8,128)} async-done(((f32[1,128,128]{2,1,0:T(8,128)}), f32[32,128,128]{2,1,0:T(8,128)}) %all-gather.6.cloned.1.call-update) | async-done | bytes 2097168 | tf_op jit(solution)/shard_map/all_gather | solution.py:25
  398.3 63.2 %while.64 = (s32[]{:T(128)}, f32[128,128]{0,1:T(8,128)S(1)}, s32[]{:T(128)}, f32[32,128,128]{2,1,0:T(8,128)}, f32[32,128,128]{2,1,0:T(8,128)}, /*index=5*/s32[]{:T(128)}, s32[]{:T(128)}) while((s32[]{:T(128)}, f32[128,128]{0,1:T(8,128)S(1)}, s32[]{:T(128)}, f32[32,128,128]{2,1,0:T(8,128)}, f32[32,128,128]{2,1,0:T(8,128)}, ...), condition=%wide.region_8.9_spmd.clone, body=%wide.region_7.8_spmd.clone.sunk | while | flops 25231364 | bytes 723043 | solution.py:34
  399.3 1.1 fusion.161
  413.5 1.1 fusion.161
  415.6 1.1 fusion.161
  429.8 1.1 fusion.161
  431.9 1.1 fusion.161
  446.1 1.1 fusion.161
  461.8 17.8 %all_gather.59 = bf16[128,2048]{1,0:T(8,128)(2,1)S(1)} all-gather(bf16[128,256]{1,0:T(8,128)(2,1)S(1)} %get-tuple-element.722), channel_id=1, replica_groups=mesh['sec'=32,'blk'=8] {'blk'}, dimensions={1}, use_global_device_ids=true | all-gather | bytes 589824 | tf_op jit(solution)/shard_map/all_gather | solution.py:101
  480.8 57.6 %all-reduce.13.cloned.1.call-done = f32[1,128,128]{2,1,0:T(8,128)} async-done(((f32[1,128,128]{2,1,0:T(8,128)}), f32[1,128,128]{2,1,0:T(8,128)}) %all-reduce.13.cloned.1.call-update) | async-done | bytes 65552 | tf_op jit(solution)/shard_map/psum | solution.py:103
  539.3 3.1 collective-permute-start.2
  542.9 1.3 collective-permute-start.3
  544.4 4.2 collective-permute-done.3
  549.1 83.2 %psum.110 = f32[1,128]{1,0:T(1,128)S(1)} all-reduce(f32[1,128]{1,0:T(1,128)S(1)} %bitcast.287), channel_id=1, replica_groups=mesh['sec'=32,'blk'=8] {'sec','blk'}, use_global_device_ids=true, to_apply=%region_11.12 | all-reduce | flops 128 | bytes 1024 | tf_op jit(solution)/shard_map/psum | solution.py:149
  632.5 72.3 %psum.111 = f32[128]{0:T(128)S(1)} all-reduce(f32[128]{0:T(128)S(1)} %get-tuple-element.687), channel_id=1, replica_groups=mesh['sec'=32,'blk'=8] {'sec','blk'}, use_global_device_ids=true, to_apply=%region_13.14 | all-reduce | flops 128 | bytes 1024 | tf_op jit(solution)/shard_map/psum | solution.py:121
  705.0 13.6 all_gather.60
  720.1 58.5 %all-reduce.15.cloned.1.call-done = f32[1,128,128]{2,1,0:T(8,128)} async-done(((f32[1,128,128]{2,1,0:T(8,128)}), f32[1,128,128]{2,1,0:T(8,128)}) %all-reduce.15.cloned.1.call-update) | async-done | bytes 65552 | tf_op jit(solution)/shard_map/psum | solution.py:138
  778.7 77.7 %all-gather.8.cloned.1.call-done = f32[32,128,128]{2,1,0:T(8,128)} async-done(((f32[1,128,128]{2,1,0:T(8,128)}), f32[32,128,128]{2,1,0:T(8,128)}) %all-gather.8.cloned.1.call-update) | async-done | bytes 2097168 | tf_op jit(solution)/shard_map/all_gather | solution.py:25
  856.4 63.2 %while.65 = (s32[]{:T(128)}, f32[128,128]{0,1:T(8,128)S(1)}, s32[]{:T(128)}, f32[32,128,128]{2,1,0:T(8,128)}, f32[32,128,128]{2,1,0:T(8,128)}, /*index=5*/s32[]{:T(128)}, s32[]{:T(128)}) while((s32[]{:T(128)}, f32[128,128]{0,1:T(8,128)S(1)}, s32[]{:T(128)}, f32[32,128,128]{2,1,0:T(8,128)}, f32[32,128,128]{2,1,0:T(8,128)}, ...), condition=%wide.region_16.17_spmd.clone, body=%wide.region_15.16_spmd.clone.sunk | while | flops 25231364 | bytes 723043 | solution.py:34
  863.4 1.1 fusion.164
  871.6 1.1 fusion.164
  879.8 1.1 fusion.164
  887.9 1.1 fusion.164
  896.1 1.1 fusion.164
  904.2 1.1 fusion.164
  912.4 1.1 fusion.164
  920.6 17.8 %all_gather.63 = bf16[128,2048]{1,0:T(8,128)(2,1)S(1)} all-gather(bf16[128,256]{1,0:T(8,128)(2,1)S(1)} %get-tuple-element.724), channel_id=1, replica_groups=mesh['sec'=32,'blk'=8] {'blk'}, dimensions={1}, use_global_device_ids=true | all-gather | bytes 589824 | tf_op jit(solution)/shard_map/all_gather | solution.py:101
  939.7 57.4 %all-reduce.17.cloned.1.call-done = f32[1,128,128]{2,1,0:T(8,128)} async-done(((f32[1,128,128]{2,1,0:T(8,128)}), f32[1,128,128]{2,1,0:T(8,128)}) %all-reduce.17.cloned.1.call-update) | async-done | bytes 65552 | tf_op jit(solution)/shard_map/psum | solution.py:103
  998.0 3.1 collective-permute-start.4
  1001.6 1.3 collective-permute-start.5
  1003.1 4.2 collective-permute-done.5
  1007.8 83.2 %psum.114 = f32[2,128]{1,0:T(2,128)S(1)} all-reduce(f32[2,128]{1,0:T(2,128)S(1)} %multiply_reduce_fusion.3), channel_id=1, replica_groups=mesh['sec'=32,'blk'=8] {'sec','blk'}, use_global_device_ids=true, to_apply=%region_19.20 | all-reduce | flops 256 | bytes 2048 | tf_op jit(solution)/shard_map/psum | solution.py:149
  1091.2 72.3 %psum.115 = f32[128]{0:T(128)S(1)} all-reduce(f32[128]{0:T(128)S(1)} %get-tuple-element.683), channel_id=1, replica_groups=mesh['sec'=32,'blk'=8] {'sec','blk'}, use_global_device_ids=true, to_apply=%region_22.23 | all-reduce | flops 128 | bytes 1024 | tf_op jit(solution)/shard_map/psum | solution.py:121
  1163.7 13.6 all_gather.64
  1178.8 58.5 %all-reduce.19.cloned.1.call-done = f32[1,128,128]{2,1,0:T(8,128)} async-done(((f32[1,128,128]{2,1,0:T(8,128)}), f32[1,128,128]{2,1,0:T(8,128)}) %all-reduce.19.cloned.1.call-update) | async-done | bytes 65552 | tf_op jit(solution)/shard_map/psum | solution.py:138
  1242.6 1.2 scatter.30
  1243.8 71.1 %all-gather.10.cloned.1.call-done = f32[32,128,128]{2,1,0:T(8,128)} async-done(((f32[1,128,128]{2,1,0:T(8,128)}), f32[32,128,128]{2,1,0:T(8,128)}) %all-gather.10.cloned.1.call-update) | async-done | bytes 2097168 | tf_op jit(solution)/shard_map/all_gather | solution.py:25
  1314.9 63.2 %while.66 = (s32[]{:T(128)}, f32[128,128]{0,1:T(8,128)S(1)}, s32[]{:T(128)}, f32[32,128,128]{2,1,0:T(8,128)}, f32[32,128,128]{2,1,0:T(8,128)}, /*index=5*/s32[]{:T(128)}, s32[]{:T(128)}) while((s32[]{:T(128)}, f32[128,128]{0,1:T(8,128)S(1)}, s32[]{:T(128)}, f32[32,128,128]{2,1,0:T(8,128)}, f32[32,128,128]{2,1,0:T(8,128)}, ...), condition=%wide.region_26.27_spmd.clone, body=%wide.region_25.26_spmd.clone.sunk | while | flops 25231364 | bytes 723043 | solution.py:34
  1379.1 17.8 %all_gather.67 = bf16[128,2048]{1,0:T(8,128)(2,1)S(1)} all-gather(bf16[128,256]{1,0:T(8,128)(2,1)S(1)} %get-tuple-element.726), channel_id=1, replica_groups=mesh['sec'=32,'blk'=8] {'blk'}, dimensions={1}, use_global_device_ids=true | all-gather | bytes 589824 | tf_op jit(solution)/shard_map/all_gather | solution.py:101
  1398.0 57.6 %all-reduce.21.cloned.1.call-done = f32[1,128,128]{2,1,0:T(8,128)} async-done(((f32[1,128,128]{2,1,0:T(8,128)}), f32[1,128,128]{2,1,0:T(8,128)}) %all-reduce.21.cloned.1.call-update) | async-done | bytes 65552 | tf_op jit(solution)/shard_map/psum | solution.py:103
  1456.6 3.2 collective-permute-start.6
  1460.3 1.3 collective-permute-start.7
  1461.8 4.2 collective-permute-done.7
  1467.2 83.2 %psum.118 = f32[3,128]{1,0:T(4,128)S(1)} all-reduce(f32[3,128]{1,0:T(4,128)S(1)} %multiply_reduce_fusion.1), channel_id=1, replica_groups=mesh['sec'=32,'blk'=8] {'sec','blk'}, use_global_device_ids=true, to_apply=%region_29.30 | all-reduce | flops 384 | bytes 3072 | tf_op jit(solution)/shard_map/psum | solution.py:149
  1550.6 72.3 %psum.119 = f32[128]{0:T(128)S(1)} all-reduce(f32[128]{0:T(128)S(1)} %multiply_reduce_fusion.4), channel_id=1, replica_groups=mesh['sec'=32,'blk'=8] {'sec','blk'}, use_global_device_ids=true, to_apply=%region_32.33 | all-reduce | flops 128 | bytes 1024 | tf_op jit(solution)/shard_map/psum | solution.py:121
  1623.0 1.9 broadcast_select_fusion
  1624.9 1.3 scatter.34
  1626.4 1.8 fusion.80
  1628.2 1.8 broadcast_select_fusion.2
  1630.1 1.8 fusion.76
  1631.9 1.7 add_add_fusion
  (489 shorter events, 200.4 us)
Async XLA Ops:
  6.5 33.7 %copy-start = (bf16[256,2048]{1,0:T(8,128)(2,1)S(1)}, bf16[256,2048]{1,0:T(8,128)(2,1)}, u32[]{:S(2)}) copy-start(bf16[256,2048]{1,0:T(8,128)(2,1)} %param.62) | copy-start | bytes 3145732
  6.5 20.0 %copy-start.1 = (bf16[256,2048]{1,0:T(8,128)(2,1)S(1)}, bf16[256,2048]{1,0:T(8,128)(2,1)}, u32[]{:S(2)}) copy-start(bf16[256,2048]{1,0:T(8,128)(2,1)} %param.61) | copy-start | bytes 3145732
  6.5 20.6 %copy-start.3 = (bf16[256,128]{1,0:T(8,128)(2,1)S(1)}, bf16[256,128]{1,0:T(8,128)(2,1)}, u32[]{:S(2)}) copy-start(bf16[256,128]{1,0:T(8,128)(2,1)} %param.63) | copy-start | bytes 196612
  6.5 68.7 %all-reduce.11.cloned.1.call-start = ((), (), s32[]{:S(2)}) async-start(), calls=%async_computation | async-start | bytes 131072 | tf_op jit(solution)/shard_map/psum | solution.py:103
  9.3 233.5 %all-reduce.23.cloned.1.call-start = ((), (), s32[]{:S(2)}) async-start(), calls=%async_computation.10 | async-start | bytes 262144 | tf_op jit(solution)/shard_map/psum | solution.py:82
  26.6 52.7 %copy-start.9 = (s32[1,128]{1,0:T(1,128)S(1)}, s32[1,128]{1,0:T(1,128)}, u32[]{:S(2)}) copy-start(s32[1,128]{1,0:T(1,128)} %param.65) | copy-start | bytes 1540
  26.6 59.3 %copy-start.2 = (f32[128,256]{1,0:T(8,128)S(1)}, f32[128,256]{1,0:T(8,128)}, u32[]{:S(2)}) copy-start(f32[128,256]{1,0:T(8,128)} %param.58) | copy-start | bytes 393220
  26.6 59.3 %copy-start.8 = (f32[128,256]{1,0:T(8,128)S(1)}, f32[128,256]{1,0:T(8,128)}, u32[]{:S(2)}) copy-start(f32[128,256]{1,0:T(8,128)} %param.59) | copy-start | bytes 393220
  26.6 59.3 %copy-start.10 = (f32[256]{0:T(256)S(1)}, f32[256]{0:T(256)}, u32[]{:S(2)}) copy-start(f32[256]{0:T(256)} %param.60) | copy-start | bytes 3076
  76.1 5.4 collective-permute-start
  80.2 5.7 collective-permute-start.1
  169.6 228.7 %copy-start.11 = (f32[128]{0:T(128)}, f32[128]{0:T(128)S(1)}, u32[]{:S(2)}) copy-start(f32[128]{0:T(128)S(1)} %psum.106) | copy-start | bytes 1540
  185.0 135.7 %all-gather.12.cloned.1.call-start = ((), (), s32[]{:S(2)}) async-start(), calls=%async_computation.9 | async-start | bytes 2162688 | tf_op jit(solution)/shard_map/all_gather | solution.py:25
  244.3 154.0 %all-gather.6.cloned.1.call-start = ((), (), s32[]{:S(2)}) async-start(), calls=%async_computation.1 | async-start | bytes 2162688 | tf_op jit(solution)/shard_map/all_gather | solution.py:25
  244.9 293.6 %all-reduce.13.cloned.1.call-start = ((), (), s32[]{:S(2)}) async-start(), calls=%async_computation.2 | async-start | bytes 131072 | tf_op jit(solution)/shard_map/psum | solution.py:103
  398.3 81.4 %copy-start.7 = (bf16[256,128]{1,0:T(8,128)(2,1)S(1)}, bf16[256,128]{1,0:T(8,128)(2,1)}, u32[]{:S(2)}) copy-start(bf16[256,128]{1,0:T(8,128)(2,1)} %param.64) | copy-start | bytes 196612
  480.4 298.2 %all-reduce.15.cloned.1.call-start = ((), (), s32[]{:S(2)}) async-start(), calls=%async_computation.3 | async-start | bytes 131072 | tf_op jit(solution)/shard_map/psum | solution.py:138
  539.3 4.9 collective-permute-start.2
  542.9 5.7 collective-permute-start.3
  720.0 136.3 %all-gather.8.cloned.1.call-start = ((), (), s32[]{:S(2)}) async-start(), calls=%async_computation.4 | async-start | bytes 2162688 | tf_op jit(solution)/shard_map/all_gather | solution.py:25
  778.6 218.5 %all-reduce.17.cloned.1.call-start = ((), (), s32[]{:S(2)}) async-start(), calls=%async_computation.5 | async-start | bytes 131072 | tf_op jit(solution)/shard_map/psum | solution.py:103
  939.1 298.2 %all-reduce.19.cloned.1.call-start = ((), (), s32[]{:S(2)}) async-start(), calls=%async_computation.6 | async-start | bytes 131072 | tf_op jit(solution)/shard_map/psum | solution.py:138
  997.1 10.2 copy-start.4
  998.0 4.9 collective-permute-start.4
  1001.6 5.7 collective-permute-start.5
  1178.8 136.2 %all-gather.10.cloned.1.call-start = ((), (), s32[]{:S(2)}) async-start(), calls=%async_computation.7 | async-start | bytes 2162688 | tf_op jit(solution)/shard_map/all_gather | solution.py:25
  1237.3 218.3 %all-reduce.21.cloned.1.call-start = ((), (), s32[]{:S(2)}) async-start(), calls=%async_computation.8 | async-start | bytes 131072 | tf_op jit(solution)/shard_map/psum | solution.py:103
  1455.7 10.3 copy-start.6
  1456.6 175.3 %copy-start.5 = (f32[128,256]{1,0:T(8,128)S(1)}, f32[128,256]{1,0:T(8,128)}, u32[]{:S(2)}) copy-start(f32[128,256]{1,0:T(8,128)} %get-tuple-element.725) | copy-start | bytes 393220
  1456.6 5.0 collective-permute-start.6
  1460.3 5.7 collective-permute-start.7
Sparse Core Ops, SparseCore 0:
  9.7 65.5 all-reduce.10
  185.1 57.6 all-reduce.22
  245.4 75.2 all-gather.11
  323.1 75.1 all-gather.5
  480.5 57.8 all-reduce.12
  720.2 58.4 all-reduce.14
  781.2 75.1 all-gather.7
  939.3 57.8 all-reduce.16
  1178.9 58.4 all-reduce.18
  1239.8 75.1 all-gather.9
  1397.8 57.8 all-reduce.20
where the time goes:
time: 1650 us; the launch traced here: 1640 us
  waiting for transfers between devices  702 us (43%)
  blocking collectives  674 us (41%)
  matrix products  116 us (7%)
  local copies, waits for them, and re-layouts  91.5 us (6%)
  other arithmetic  20.7 us (1%)
  starting transfers between devices  18.2 us (1%)
    all_gather x4, waiting for transfers between devices, entering(): pieces = jax.tree.map(lambda part: lax.all_gather(part, axis), value)  302 us
    psum x4, blocking collectives, lengths(): lax.psum(jnp.sum(vector * vector, axis=1), ('sec', 'blk')) + epsilon  300 us
    psum x3, blocking collectives, local(): lax.psum(jnp.sum(product[None] * stacked, axis=2), ('sec', 'blk'))  250 us
    psum x4, waiting for transfers between devices, operator(): lax.psum(jnp.dot(rounded, ahead_panel, preferred_element_type=jnp.float32...  207 us
    psum x2, waiting for transfers between devices, local(): lax.psum(jnp.dot(precondition_folded, selector, precision=highest), 'blk')  117 us
    dot_general x93, matrix products, compose(): jnp.dot(first_value, second_map.T, precision=highest) + second_value  97.7 us
    dynamic_slice x186, local copies, waits for them, and re-layouts, step(): longer = join(so_far, jax.tree.map(lambda part: part[position], pieces))  87 us
    all_gather x4, blocking collectives, operator(): lax.all_gather(rounded, 'blk', axis=1, tiled=True)  69.6 us
  transfers between devices with their start and end apart: 19, of which 15 were waited for; matrix products, arithmetic and copies ran while one was open for 1% of the time, Pallas kernels for 0%

commit v1 on v0

--- a/solution.py
+++ b/solution.py
@@ -79,7 +79,9 @@
         lax.all_gather(back_panel, "blk", axis=0, tiled=True),
         preferred_element_type=jnp.float32,
     )
-    panel_maps = -lax.psum(jnp.dot(selector.T, gain_panel, precision=highest), "blk")
+    panel_maps = -jnp.sum(
+        lax.all_gather(jnp.dot(selector.T, gain_panel, precision=highest), "blk"), axis=0
+    )
 
     def section_terms(dense_part, behind_vals, piece):
         width = piece.shape[1]

time: 1650 us -> 1590 us (0.964)
  waiting for transfers between devices: 702 us -> 631 us
    psum x1 -> x0, waiting for transfers between devices: 57.8 us -> none  [local(): lax.psum(jnp.dot(selector.T, gain_panel, precision=highest), 'blk')]
    all_gather x4, waiting for transfers between devices: 302 us -> 245 us  [entering(): pieces = jax.tree.map(lambda part: lax.all_gather(part, axis), value)]
    psum x2 -> x3, waiting for transfers between devices: 117 us -> 161 us  [local(): lax.psum(jnp.dot(precondition_folded, selector, precision=highest), 'blk')]
where the time goes in v1:
time: 1590 us; the launch traced here: 1580 us
  blocking collectives  689 us (43%)
  waiting for transfers between devices  631 us (40%)
  matrix products  116 us (7%)
  local copies, waits for them, and re-layouts  91.5 us (6%)
  other arithmetic  19.9 us (1%)
  starting transfers between devices  18 us (1%)
    psum x4, blocking collectives, lengths(): lax.psum(jnp.sum(vector * vector, axis=1), ('sec', 'blk')) + epsilon  300 us
    psum x3, blocking collectives, local(): lax.psum(jnp.sum(product[None] * stacked, axis=2), ('sec', 'blk'))  250 us
    all_gather x4, waiting for transfers between devices, entering(): pieces = jax.tree.map(lambda part: lax.all_gather(part, axis), value)  245 us
    psum x4, waiting for transfers between devices, operator(): lax.psum(jnp.dot(rounded, ahead_panel, preferred_element_type=jnp.float32...  208 us
    psum x3, waiting for transfers between devices, local(): lax.psum(jnp.dot(precondition_folded, selector, precision=highest), 'blk')  161 us
    dot_general x93, matrix products, compose(): jnp.dot(first_value, second_map.T, precision=highest) + second_value  97.7 us
    dynamic_slice x186, local copies, waits for them, and re-layouts, step(): longer = join(so_far, jax.tree.map(lambda part: part[position], pieces))  87 us
    all_gather x4, blocking collectives, operator(): lax.all_gather(rounded, 'blk', axis=1, tiled=True)  71.7 us
  transfers between devices with their start and end apart: 19, of which 15 were waited for; matrix products, arithmetic and copies ran while one was open for 1% of the time, Pallas kernels for 0%

profile of v1, /device:TPU:1, one launch (start us, length us, event | category | flops | bytes accessed | tf_op | source)
XLA Modules:
  0.0 1584.8 jit_solution(2553236849434176790)
XLA Ops:
  7.4 1.1 convert_element_type.42
  8.5 1.7 convolution_bitcast_fusion.13
  10.2 16.2 %all_gather.56 = bf16[128,2048]{1,0:T(8,128)(2,1)S(1)} all-gather(bf16[128,256]{1,0:T(8,128)(2,1)S(1)} %convert_element_type.42), channel_id=1, replica_groups=mesh['sec'=32,'blk'=8] {'blk'}, dimensions={1}, use_global_device_ids=true | all-gather | bytes 589824 | tf_op jit(solution)/shard_map/all_gather | solution.py:103
  28.0 13.1 all_gather.58
  41.6 34.5 %all-reduce.10.cloned.1.call-done = f32[1,128,128]{1,2,0:T(8,128)} async-done(((f32[1,128,128]{1,2,0:T(8,128)}), f32[1,128,128]{1,2,0:T(8,128)}) %all-reduce.10.cloned.1.call-update) | async-done | bytes 65552 | tf_op jit(solution)/shard_map/psum | solution.py:105
  77.0 3.1 collective-permute-start
  80.4 1.3 collective-permute-start.1
  81.9 4.2 collective-permute-done.1
  86.5 83.2 %psum.99 = f32[128]{0:T(128)S(1)} all-reduce(f32[128]{0:T(128)S(1)} %get-tuple-element.718), channel_id=1, replica_groups=mesh['sec'=32,'blk'=8] {'sec','blk'}, use_global_device_ids=true, to_apply=%region_4.0 | all-reduce | flops 128 | bytes 1024 | tf_op jit(solution)/shard_map/psum | solution.py:123
  169.9 13.9 all_gather.57
  185.2 13.1 all-gather
  199.1 43.5 %all-reduce.12.cloned.1.call-done = f32[1,128,128]{2,1,0:T(8,128)} async-done(((f32[1,128,128]{2,1,0:T(8,128)}), f32[1,128,128]{2,1,0:T(8,128)}) %all-reduce.12.cloned.1.call-update) | async-done | bytes 65552 | tf_op jit(solution)/shard_map/psum | solution.py:140
  242.7 25.0 %all-gather.13.cloned.1.call-done = f32[4096,128]{1,0:T(8,128)} async-done(((f32[128,128]{1,0:T(8,128)}), f32[4096,128]{1,0:T(8,128)}) %all-gather.13.cloned.1.call-update) | async-done | bytes 2097168 | tf_op jit(solution)/shard_map/all_gather | solution.py:25
  267.7 77.8 %all-gather.7.cloned.1.call-done = f32[32,128,128]{2,1,0:T(8,128)} async-done(((f32[1,128,128]{2,1,0:T(8,128)}), f32[32,128,128]{2,1,0:T(8,128)}) %all-gather.7.cloned.1.call-update) | async-done | bytes 2097168 | tf_op jit(solution)/shard_map/all_gather | solution.py:25
  345.5 63.2 %while.64 = (s32[]{:T(128)}, f32[128,128]{0,1:T(8,128)S(1)}, s32[]{:T(128)}, f32[32,128,128]{2,1,0:T(8,128)}, f32[32,128,128]{2,1,0:T(8,128)}, /*index=5*/s32[]{:T(128)}, s32[]{:T(128)}) while((s32[]{:T(128)}, f32[128,128]{0,1:T(8,128)S(1)}, s32[]{:T(128)}, f32[32,128,128]{2,1,0:T(8,128)}, f32[32,128,128]{2,1,0:T(8,128)}, ...), condition=%wide.region_8.9_spmd.clone, body=%wide.region_7.8_spmd.clone.sunk | while | flops 25231364 | bytes 723043 | solution.py:34
  350.6 1.1 fusion.161
  352.6 1.1 fusion.161
  366.9 1.1 fusion.161
  409.0 18.5 %all_gather.64 = bf16[128,2048]{1,0:T(8,128)(2,1)S(1)} all-gather(bf16[128,256]{1,0:T(8,128)(2,1)S(1)} %get-tuple-element.720), channel_id=1, replica_groups=mesh['sec'=32,'blk'=8] {'blk'}, dimensions={1}, use_global_device_ids=true | all-gather | bytes 589824 | tf_op jit(solution)/shard_map/all_gather | solution.py:103
  428.7 57.8 %all-reduce.14.cloned.1.call-done = f32[1,128,128]{2,1,0:T(8,128)} async-done(((f32[1,128,128]{2,1,0:T(8,128)}), f32[1,128,128]{2,1,0:T(8,128)}) %all-reduce.14.cloned.1.call-update) | async-done | bytes 65552 | tf_op jit(solution)/shard_map/psum | solution.py:105
  487.4 3.1 collective-permute-start.2
  490.9 1.3 collective-permute-start.3
  492.4 4.2 collective-permute-done.3
  497.2 83.2 %psum.102 = f32[1,128]{1,0:T(1,128)S(1)} all-reduce(f32[1,128]{1,0:T(1,128)S(1)} %bitcast.289), channel_id=1, replica_groups=mesh['sec'=32,'blk'=8] {'sec','blk'}, use_global_device_ids=true, to_apply=%region_11.12 | all-reduce | flops 128 | bytes 1024 | tf_op jit(solution)/shard_map/psum | solution.py:151
  580.6 72.3 %psum.103 = f32[128]{0:T(128)S(1)} all-reduce(f32[128]{0:T(128)S(1)} %get-tuple-element.685), channel_id=1, replica_groups=mesh['sec'=32,'blk'=8] {'sec','blk'}, use_global_device_ids=true, to_apply=%region_13.14 | all-reduce | flops 128 | bytes 1024 | tf_op jit(solution)/shard_map/psum | solution.py:123
  653.0 13.6 all_gather.65
  668.1 58.5 %all-reduce.16.cloned.1.call-done = f32[1,128,128]{2,1,0:T(8,128)} async-done(((f32[1,128,128]{2,1,0:T(8,128)}), f32[1,128,128]{2,1,0:T(8,128)}) %all-reduce.16.cloned.1.call-update) | async-done | bytes 65552 | tf_op jit(solution)/shard_map/psum | solution.py:140
  726.7 74.4 %all-gather.9.cloned.1.call-done = f32[32,128,128]{2,1,0:T(8,128)} async-done(((f32[1,128,128]{2,1,0:T(8,128)}), f32[32,128,128]{2,1,0:T(8,128)}) %all-gather.9.cloned.1.call-update) | async-done | bytes 2097168 | tf_op jit(solution)/shard_map/all_gather | solution.py:25
  801.2 63.2 %while.65 = (s32[]{:T(128)}, f32[128,128]{0,1:T(8,128)S(1)}, s32[]{:T(128)}, f32[32,128,128]{2,1,0:T(8,128)}, f32[32,128,128]{2,1,0:T(8,128)}, /*index=5*/s32[]{:T(128)}, s32[]{:T(128)}) while((s32[]{:T(128)}, f32[128,128]{0,1:T(8,128)S(1)}, s32[]{:T(128)}, f32[32,128,128]{2,1,0:T(8,128)}, f32[32,128,128]{2,1,0:T(8,128)}, ...), condition=%wide.region_16.17_spmd.clone, body=%wide.region_15.16_spmd.clone.sunk | while | flops 25231364 | bytes 723043 | solution.py:34
  806.2 1.1 fusion.164
  808.3 1.1 fusion.164
  812.3 1.1 fusion.164
  814.4 1.1 fusion.164
  820.5 1.1 fusion.164
  828.7 1.1 fusion.164
  836.8 1.1 fusion.164
  845.0 1.1 fusion.164
  853.1 1.1 fusion.164
  861.3 1.1 fusion.164
  865.4 18.6 %all_gather.68 = bf16[128,2048]{1,0:T(8,128)(2,1)S(1)} all-gather(bf16[128,256]{1,0:T(8,128)(2,1)S(1)} %get-tuple-element.722), channel_id=1, replica_groups=mesh['sec'=32,'blk'=8] {'blk'}, dimensions={1}, use_global_device_ids=true | all-gather | bytes 589824 | tf_op jit(solution)/shard_map/all_gather | solution.py:103
  885.2 57.7 %all-reduce.18.cloned.1.call-done = f32[1,128,128]{2,1,0:T(8,128)} async-done(((f32[1,128,128]{2,1,0:T(8,128)}), f32[1,128,128]{2,1,0:T(8,128)}) %all-reduce.18.cloned.1.call-update) | async-done | bytes 65552 | tf_op jit(solution)/shard_map/psum | solution.py:105
  943.9 3.1 collective-permute-start.4
  947.5 1.3 collective-permute-start.5
  948.9 4.2 collective-permute-done.5
  953.6 83.2 %psum.106 = f32[2,128]{1,0:T(2,128)S(1)} all-reduce(f32[2,128]{1,0:T(2,128)S(1)} %multiply_reduce_fusion.3), channel_id=1, replica_groups=mesh['sec'=32,'blk'=8] {'sec','blk'}, use_global_device_ids=true, to_apply=%region_19.20 | all-reduce | flops 256 | bytes 2048 | tf_op jit(solution)/shard_map/psum | solution.py:151
  1037.1 72.3 %psum.107 = f32[128]{0:T(128)S(1)} all-reduce(f32[128]{0:T(128)S(1)} %get-tuple-element.681), channel_id=1, replica_groups=mesh['sec'=32,'blk'=8] {'sec','blk'}, use_global_device_ids=true, to_apply=%region_22.23 | all-reduce | flops 128 | bytes 1024 | tf_op jit(solution)/shard_map/psum | solution.py:123
  1109.5 13.6 all_gather.69
  1124.6 58.5 %all-reduce.20.cloned.1.call-done = f32[1,128,128]{2,1,0:T(8,128)} async-done(((f32[1,128,128]{2,1,0:T(8,128)}), f32[1,128,128]{2,1,0:T(8,128)}) %all-reduce.20.cloned.1.call-update) | async-done | bytes 65552 | tf_op jit(solution)/shard_map/psum | solution.py:140
  1188.5 1.2 scatter.30
  1189.7 68.0 %all-gather.11.cloned.1.call-done = f32[32,128,128]{2,1,0:T(8,128)} async-done(((f32[1,128,128]{2,1,0:T(8,128)}), f32[32,128,128]{2,1,0:T(8,128)}) %all-gather.11.cloned.1.call-update) | async-done | bytes 2097168 | tf_op jit(solution)/shard_map/all_gather | solution.py:25
  1257.7 63.2 %while.66 = (s32[]{:T(128)}, f32[128,128]{0,1:T(8,128)S(1)}, s32[]{:T(128)}, f32[32,128,128]{2,1,0:T(8,128)}, f32[32,128,128]{2,1,0:T(8,128)}, /*index=5*/s32[]{:T(128)}, s32[]{:T(128)}) while((s32[]{:T(128)}, f32[128,128]{0,1:T(8,128)S(1)}, s32[]{:T(128)}, f32[32,128,128]{2,1,0:T(8,128)}, f32[32,128,128]{2,1,0:T(8,128)}, ...), condition=%wide.region_26.27_spmd.clone, body=%wide.region_25.26_spmd.clone.sunk | while | flops 25231364 | bytes 723043 | solution.py:34
  1321.8 18.5 %all_gather.72 = bf16[128,2048]{1,0:T(8,128)(2,1)S(1)} all-gather(bf16[128,256]{1,0:T(8,128)(2,1)S(1)} %get-tuple-element.724), channel_id=1, replica_groups=mesh['sec'=32,'blk'=8] {'blk'}, dimensions={1}, use_global_device_ids=true | all-gather | bytes 589824 | tf_op jit(solution)/shard_map/all_gather | solution.py:103
  1341.4 57.8 %all-reduce.22.cloned.1.call-done = f32[1,128,128]{2,1,0:T(8,128)} async-done(((f32[1,128,128]{2,1,0:T(8,128)}), f32[1,128,128]{2,1,0:T(8,128)}) %all-reduce.22.cloned.1.call-update) | async-done | bytes 65552 | tf_op jit(solution)/shard_map/psum | solution.py:105
  1400.2 3.2 collective-permute-start.6
  1403.9 1.3 collective-permute-start.7
  1405.3 4.2 collective-permute-done.7
  1410.7 83.2 %psum.110 = f32[3,128]{1,0:T(4,128)S(1)} all-reduce(f32[3,128]{1,0:T(4,128)S(1)} %multiply_reduce_fusion.1), channel_id=1, replica_groups=mesh['sec'=32,'blk'=8] {'sec','blk'}, use_global_device_ids=true, to_apply=%region_29.30 | all-reduce | flops 384 | bytes 3072 | tf_op jit(solution)/shard_map/psum | solution.py:151
  1494.2 72.3 %psum.111 = f32[128]{0:T(128)S(1)} all-reduce(f32[128]{0:T(128)S(1)} %multiply_reduce_fusion.4), channel_id=1, replica_groups=mesh['sec'=32,'blk'=8] {'sec','blk'}, use_global_device_ids=true, to_apply=%region_32.33 | all-reduce | flops 128 | bytes 1024 | tf_op jit(solution)/shard_map/psum | solution.py:123
  1566.5 1.9 broadcast_select_fusion
  1568.5 1.3 scatter.34
  1569.9 1.8 fusion.80
  1571.8 1.8 broadcast_select_fusion.2
  1573.6 1.8 fusion.76
  1575.5 1.7 add_add_fusion
  (491 shorter events, 199.7 us)
Async XLA Ops:
  7.4 33.7 %copy-start = (bf16[256,2048]{1,0:T(8,128)(2,1)S(1)}, bf16[256,2048]{1,0:T(8,128)(2,1)}, u32[]{:S(2)}) copy-start(bf16[256,2048]{1,0:T(8,128)(2,1)} %param.62) | copy-start | bytes 3145732
  7.4 20.0 %copy-start.1 = (bf16[256,2048]{1,0:T(8,128)(2,1)S(1)}, bf16[256,2048]{1,0:T(8,128)(2,1)}, u32[]{:S(2)}) copy-start(bf16[256,2048]{1,0:T(8,128)(2,1)} %param.61) | copy-start | bytes 3145732
  7.4 20.6 %copy-start.3 = (bf16[256,128]{1,0:T(8,128)(2,1)S(1)}, bf16[256,128]{1,0:T(8,128)(2,1)}, u32[]{:S(2)}) copy-start(bf16[256,128]{1,0:T(8,128)(2,1)} %param.63) | copy-start | bytes 196612
  7.4 68.7 %all-reduce.10.cloned.1.call-start = ((), (), s32[]{:S(2)}) async-start(), calls=%async_computation | async-start | bytes 131072 | tf_op jit(solution)/shard_map/psum | solution.py:105
  10.2 232.5 %all-reduce.12.cloned.1.call-start = ((), (), s32[]{:S(2)}) async-start(), calls=%async_computation.1 | async-start | bytes 131072 | tf_op jit(solution)/shard_map/psum | solution.py:140
  27.4 52.6 %copy-start.9 = (s32[1,128]{1,0:T(1,128)S(1)}, s32[1,128]{1,0:T(1,128)}, u32[]{:S(2)}) copy-start(s32[1,128]{1,0:T(1,128)} %param.65) | copy-start | bytes 1540
  27.4 58.7 %copy-start.2 = (f32[128,256]{1,0:T(8,128)S(1)}, f32[128,256]{1,0:T(8,128)}, u32[]{:S(2)}) copy-start(f32[128,256]{1,0:T(8,128)} %param.58) | copy-start | bytes 393220
  27.4 58.7 %copy-start.8 = (f32[128,256]{1,0:T(8,128)S(1)}, f32[128,256]{1,0:T(8,128)}, u32[]{:S(2)}) copy-start(f32[128,256]{1,0:T(8,128)} %param.59) | copy-start | bytes 393220
  27.4 58.7 %copy-start.10 = (f32[256]{0:T(256)S(1)}, f32[256]{0:T(256)}, u32[]{:S(2)}) copy-start(f32[256]{0:T(256)} %param.60) | copy-start | bytes 3076
  77.0 4.7 collective-permute-start
  80.4 5.7 collective-permute-start.1
  169.8 72.9 %copy-start.11 = (f32[128]{0:T(128)}, f32[128]{0:T(128)S(1)}, u32[]{:S(2)}) copy-start(f32[128]{0:T(128)S(1)} %psum.99) | copy-start | bytes 1540
  185.2 82.5 %all-gather.13.cloned.1.call-start = ((), (), s32[]{:S(2)}) async-start(), calls=%async_computation.10 | async-start | bytes 2162688 | tf_op jit(solution)/shard_map/all_gather | solution.py:25
  199.1 146.4 %all-gather.7.cloned.1.call-start = ((), (), s32[]{:S(2)}) async-start(), calls=%async_computation.2 | async-start | bytes 2162688 | tf_op jit(solution)/shard_map/all_gather | solution.py:25
  242.7 243.8 %all-reduce.14.cloned.1.call-start = ((), (), s32[]{:S(2)}) async-start(), calls=%async_computation.3 | async-start | bytes 131072 | tf_op jit(solution)/shard_map/psum | solution.py:105
  345.5 82.0 %copy-start.7 = (bf16[256,128]{1,0:T(8,128)(2,1)S(1)}, bf16[256,128]{1,0:T(8,128)(2,1)}, u32[]{:S(2)}) copy-start(bf16[256,128]{1,0:T(8,128)(2,1)} %param.64) | copy-start | bytes 196612
  428.3 298.3 %all-reduce.16.cloned.1.call-start = ((), (), s32[]{:S(2)}) async-start(), calls=%async_computation.4 | async-start | bytes 131072 | tf_op jit(solution)/shard_map/psum | solution.py:140
  487.4 4.9 collective-permute-start.2
  490.9 5.7 collective-permute-start.3
  668.1 133.1 %all-gather.9.cloned.1.call-start = ((), (), s32[]{:S(2)}) async-start(), calls=%async_computation.5 | async-start | bytes 2162688 | tf_op jit(solution)/shard_map/all_gather | solution.py:25
  726.7 216.3 %all-reduce.18.cloned.1.call-start = ((), (), s32[]{:S(2)}) async-start(), calls=%async_computation.6 | async-start | bytes 131072 | tf_op jit(solution)/shard_map/psum | solution.py:105
  884.8 298.3 %all-reduce.20.cloned.1.call-start = ((), (), s32[]{:S(2)}) async-start(), calls=%async_computation.7 | async-start | bytes 131072 | tf_op jit(solution)/shard_map/psum | solution.py:140
  943.0 10.2 copy-start.4
  943.9 4.9 collective-permute-start.4
  947.5 5.7 collective-permute-start.5
  1124.6 133.1 %all-gather.11.cloned.1.call-start = ((), (), s32[]{:S(2)}) async-start(), calls=%async_computation.8 | async-start | bytes 2162688 | tf_op jit(solution)/shard_map/all_gather | solution.py:25
  1183.2 216.1 %all-reduce.22.cloned.1.call-start = ((), (), s32[]{:S(2)}) async-start(), calls=%async_computation.9 | async-start | bytes 131072 | tf_op jit(solution)/shard_map/psum | solution.py:105
  1399.2 10.3 copy-start.6
  1400.1 175.3 %copy-start.5 = (f32[128,256]{1,0:T(8,128)S(1)}, f32[128,256]{1,0:T(8,128)}, u32[]{:S(2)}) copy-start(f32[128,256]{1,0:T(8,128)} %get-tuple-element.723) | copy-start | bytes 393220
  1400.2 5.0 collective-permute-start.6
  1403.9 5.7 collective-permute-start.7
Sparse Core Ops, SparseCore 0:
  10.5 65.5 all-reduce.9
  185.3 57.3 all-reduce.11
  428.4 58.0 all-reduce.13
  668.2 58.4 all-reduce.15
  884.9 58.0 all-reduce.17
  1124.7 58.4 all-reduce.19
  1341.2 58.0 all-reduce.21
Sparse Core Ops, SparseCore 1:
  199.1 68.5 all-gather.12
  270.2 75.3 all-gather.6
  726.8 74.3 all-gather.8
  1183.3 74.3 all-gather.10
